TPU v7x, 512 devices: a whole 4x4x16 slice. The times are simulated.
512 devices in a mesh: seq: 64 (over y, z), req: 8 (over x, core).
Axes of the slice: x: 4, y: 4, z: 16, core: 2. Of those that a mesh axis runs over, the one named last changes fastest.
Arguments:
- new_token_queries: bfloat16 [4, 64, 2048], P(None, 'req'), may hold values from -48 to 48
- new_token_keys: bfloat16 [4, 64, 1024], P(None, 'req'), may hold values from -48 to 48
- new_token_values: bfloat16 [4, 64, 1024], P(None, 'req'), may hold values from -6 to 6
- key_cache: bfloat16 [64, 2048, 1024], P('req', 'seq'), may hold values from -48 to 48
- value_cache: bfloat16 [64, 2048, 1024], P('req', 'seq'), may hold values from -6 to 6
- cache_len: int32 [64], P('req'), may hold values from 1 to 2048, 34816 in all
- resid: bfloat16 [4, 64, 2048], P(None, 'req'), may hold values from -6 to 6
- gain: bfloat16 [2048], replicated, may hold values from 0.5 to 1.5
- w_gate: bfloat16 [2048, 6144], P('seq', 'req'), may hold values from -0.125 to 0.125
- w_up: bfloat16 [2048, 6144], P('seq', 'req'), may hold values from -0.125 to 0.125
- w_down: bfloat16 [6144, 2048], P('req', 'seq'), may hold values from -0.078125 to 0.078125
Outputs:
- out: bfloat16 [4, 64, 2048], P(None, 'req')
All inputs are finite; a program needn't handle non-finite values. No bound on the sum of `cache_len` on one device may be relied on, other than what follows from the above.
Results may differ from a plain program's by a relative error of at most 0.006.
Values may be sent and summed in bfloat16 or wider, within the bound.
A program may use at most 128 MiB of HBM per device.

v0:
```python
import math
import jax
import jax.numpy as jnp
from jax import lax
from jax.sharding import PartitionSpec as P

QUERY_HEADS = 16
KEY_VALUE_HEADS = 8
HEAD_SIZE = 128
NEG_FILL = -1e30
EPSILON = 1e-06


def partial_softmax(q, keys, values, valid):
    scores = jnp.einsum("rkmd,rbkd->rkmb", q, keys, preferred_element_type=jnp.float32) / math.sqrt(
        HEAD_SIZE
    )
    inside = valid[:, None]
    scores = jnp.where(inside, scores, NEG_FILL)
    highest = jnp.max(scores, axis=-1)
    weights = jnp.where(inside, jnp.exp(scores - highest[..., None]), 0.0).astype(jnp.bfloat16)
    totals = jnp.sum(weights.astype(jnp.float32), axis=-1)
    weighted = jnp.einsum("rkmb,rbkd->rkmd", weights, values, preferred_element_type=jnp.float32)
    return (highest, totals, weighted)


def body(q, nk, nv, kc, vc, cache_len, resid, gain, w_gate, w_up, w_down):
    steps, rows, model = q.shape
    page = kc.shape[1]
    width = w_gate.shape[0]
    units = w_gate.shape[1]
    group = QUERY_HEADS // KEY_VALUE_HEADS
    me = lax.axis_index("seq")
    positions = me * page + jnp.arange(page, dtype=jnp.int32)
    valid = (positions[None, :] < cache_len[:, None])[:, None, :]
    qv = q.reshape(steps, rows, KEY_VALUE_HEADS, group, HEAD_SIZE).transpose(1, 2, 0, 3, 4)
    qv = qv.reshape(rows, KEY_VALUE_HEADS, steps * group, HEAD_SIZE)
    keys = kc.reshape(rows, page, KEY_VALUE_HEADS, HEAD_SIZE)
    values = vc.reshape(rows, page, KEY_VALUE_HEADS, HEAD_SIZE)
    local = partial_softmax(qv, keys, values, jnp.broadcast_to(valid, (rows, steps * group, page)))
    highest = lax.pmax(local[0], "seq")
    factor = jnp.exp(local[0] - highest)
    totals, weighted = lax.psum((factor * local[1], factor[..., None] * local[2]), "seq")
    fk = jnp.swapaxes(nk, 0, 1).reshape(rows, steps, KEY_VALUE_HEADS, HEAD_SIZE)
    fv = jnp.swapaxes(nv, 0, 1).reshape(rows, steps, KEY_VALUE_HEADS, HEAD_SIZE)
    step_of = jnp.arange(steps * group, dtype=jnp.int32) // group
    causal = jnp.arange(steps, dtype=jnp.int32)[None, :] <= step_of[:, None]
    fresh = partial_softmax(
        qv, fk, fv, jnp.broadcast_to(causal[None], (rows, steps * group, steps))
    )
    peak = jnp.maximum(highest, fresh[0])
    a = jnp.exp(highest - peak)
    b = jnp.exp(fresh[0] - peak)
    total = a * totals + b * fresh[1]
    acc = a[..., None] * weighted + b[..., None] * fresh[2]
    attn = (acc / total[..., None]).astype(jnp.bfloat16)
    attn = attn.reshape(rows, KEY_VALUE_HEADS, steps, group, HEAD_SIZE).transpose(2, 0, 1, 3, 4)
    attn = attn.reshape(steps, rows, model)
    attn = lax.optimization_barrier(attn).astype(jnp.float32)
    stream = (resid.astype(jnp.float32) + attn).astype(jnp.bfloat16)
    stream = lax.optimization_barrier(stream).astype(jnp.float32)
    scaled = lax.rsqrt(jnp.mean(stream * stream, axis=-1, keepdims=True) + EPSILON)
    normed = (stream * scaled * gain.astype(jnp.float32)).astype(jnp.bfloat16)
    own = lax.dynamic_slice_in_dim(normed, me * width, width, 2)
    every = lax.all_gather(own, "req", axis=1, tiled=True).reshape(-1, width)
    joined = jnp.concatenate([w_gate, w_up], axis=1)
    sums = lax.psum(jnp.dot(every, joined, preferred_element_type=jnp.float32), "seq")
    hidden = (jax.nn.silu(sums[:, :units]) * sums[:, units:]).astype(jnp.bfloat16)
    down = jnp.dot(hidden, w_down, preferred_element_type=jnp.float32)
    down = lax.psum_scatter(down.reshape(steps, -1, width), "req", scatter_dimension=1, tiled=True)
    piece = (lax.dynamic_slice_in_dim(stream, me * width, width, 2) + down).astype(jnp.bfloat16)
    return lax.all_gather(piece, "seq", axis=2, tiled=True)


def solution(mesh):
    placed = (
        P(None, "req", None),
        P(None, "req", None),
        P(None, "req", None),
        P("req", "seq", None),
        P("req", "seq", None),
        P("req"),
        P(None, "req", None),
        P(),
        P("seq", "req"),
        P("seq", "req"),
        P("req", "seq"),
    )
    return jax.shard_map(
        body, mesh=mesh, in_specs=placed, out_specs=P(None, "req", None), check_vma=False
    )
```

profile of v0, /device:TPU:8, one launch (start us, length us, event | category | flops | bytes accessed | tf_op | source)
XLA Modules:
  0.0 988.8 jit_solution(13132273959055247014)
XLA Ops:
  6.6 1.1 copy.49
  7.6 0.7 broadcast_compare_fusion
  8.4 1.5 fusion.27
  9.9 261.8 %pmax.7 = f32[8,8,8]{2,1,0:T(8,128)S(1)} all-reduce(f32[8,8,8]{2,1,0:T(8,128)S(1)} %get-tuple-element.10), channel_id=1, replica_groups=mesh['seq'=64,'req'=8] {'seq'}, use_global_device_ids=true, to_apply=%region_1.2 | all-reduce | flops 512 | bytes 4096 | tf_op jit(solution)/shard_map/pmax | solution.py:41
  271.6 0.3 convert_reduce_fusion
  271.9 1.0 convolution_multiply_fusion.1
  273.1 0.2 fusion.28
  273.3 0.1 convert_reduce_fusion.1
  273.4 0.8 dynamic-slice.2
  274.2 274.0 %psum.22 = f32[8,8,8]{2,1,0:T(8,128)S(1)} all-reduce(f32[8,8,8]{2,1,0:T(8,128)S(1)} %get-tuple-element.8), channel_id=1, replica_groups=mesh['seq'=64,'req'=8] {'seq'}, use_global_device_ids=true, to_apply=%region_5.6 | all-reduce | flops 512 | bytes 4096 | tf_op jit(solution)/shard_map/psum | solution.py:43
  548.3 1.4 fusion.3
  549.7 0.2 copy.54
  549.9 0.1 multiply_reduce_fusion
  550.2 13.1 %all_gather.6 = bf16[4,64,32]{2,0,1:T(4,128)(2,1)S(1)} all-gather(bf16[4,8,32]{2,0,1:T(4,128)(2,1)S(1)} %copy.55), channel_id=1, replica_groups=mesh['seq'=64,'req'=8] {'req'}, dimensions={1}, use_global_device_ids=true | all-gather | bytes 18432 | tf_op jit(solution)/shard_map/all_gather | solution.py:65
  563.5 1.5 fusion.12
  565.0 1.3 dynamic-slice
  566.9 286.0 %all-reduce.6.cloned.1.call-done = f32[256,1536]{1,0:T(8,128)} async-done(((f32[256,1536]{1,0:T(8,128)}), f32[256,1536]{1,0:T(8,128)}) %all-reduce.6.cloned.1.call-update) | async-done | bytes 1572880 | tf_op jit(solution)/shard_map/psum | solution.py:67
  852.9 1.7 fusion.10
  854.6 0.1 reshape.72
  854.7 0.1 copy.57
  854.9 24.7 %all-reduce = f32[4,64,32]{2,0,1:T(4,128)S(1)} all-reduce(f32[4,64,32]{2,0,1:T(4,128)S(1)} %copy.57), channel_id=2, replica_groups=mesh['seq'=64,'req'=8] {'req'}, use_global_device_ids=true, to_apply=%region_9.10.clone | all-reduce | flops 8192 | bytes 65536
  879.7 0.1 copy.59
  879.8 100.1 %all_gather.7 = bf16[4,8,2048]{1,0,2:T(4,128)(2,1)S(1)} all-gather(bf16[4,8,32]{1,0,2:T(4,128)(2,1)S(1)} %copy.59), channel_id=1, replica_groups=mesh['seq'=64,'req'=8] {'seq'}, dimensions={2}, use_global_device_ids=true | all-gather | bytes 133120 | tf_op jit(solution)/shard_map/all_gather | solution.py:72
  979.9 2.1 copy.60
  (33 shorter events, 0.6 us)
Async XLA Ops:
  6.5 265.4 %copy-start = (bf16[8,32,1024]{2,1,0:T(8,128)(2,1)S(1)}, bf16[8,32,1024]{2,1,0:T(8,128)(2,1)}, u32[]{:S(2)}) copy-start(bf16[8,32,1024]{2,1,0:T(8,128)(2,1)} %param.15) | copy-start | bytes 1572868
  6.5 541.8 %all-reduce.4.cloned.1.call-start = ((), (), s32[]{:S(2)}) async-start(), calls=%async_computation | async-start | bytes 524288 | tf_op jit(solution)/shard_map/psum | solution.py:43
  6.5 266.5 %copy-start.4 = (bf16[4,8,1024]{2,1,0:T(8,128)(2,1)S(1)}, bf16[4,8,1024]{2,1,0:T(8,128)(2,1)}, u32[]{:S(2)}) copy-start(bf16[4,8,1024]{2,1,0:T(8,128)(2,1)} %param.12) | copy-start | bytes 196612
  9.8 538.5 %copy-start.5 = (bf16[4,8,1024]{2,1,0:T(8,128)(2,1)S(1)}, bf16[4,8,1024]{2,1,0:T(8,128)(2,1)}, u32[]{:S(2)}) copy-start(bf16[4,8,1024]{2,1,0:T(8,128)(2,1)} %param.13) | copy-start | bytes 196612
  273.0 579.9 %all-reduce.6.cloned.1.call-start = ((), (), s32[]{:S(2)}) async-start(), calls=%async_computation.1 | async-start | bytes 3145728 | tf_op jit(solution)/shard_map/psum | solution.py:67
  273.1 276.8 %copy-start.1 = (bf16[4,8,2048]{2,1,0:T(8,128)(2,1)S(1)}, bf16[4,8,2048]{2,1,0:T(8,128)(2,1)}, u32[]{:S(2)}) copy-start(bf16[4,8,2048]{2,1,0:T(8,128)(2,1)} %param.17) | copy-start | bytes 393220
  548.3 15.1 %copy-start.2 = (bf16[32,768]{1,0:T(8,128)(2,1)S(1)}, bf16[32,768]{1,0:T(8,128)(2,1)}, u32[]{:S(2)}) copy-start(bf16[32,768]{1,0:T(8,128)(2,1)} %param.20) | copy-start | bytes 147460
  548.3 15.1 %copy-start.3 = (bf16[32,768]{1,0:T(8,128)(2,1)S(1)}, bf16[32,768]{1,0:T(8,128)(2,1)}, u32[]{:S(2)}) copy-start(bf16[32,768]{1,0:T(8,128)(2,1)} %param.19) | copy-start | bytes 147460
  563.4 289.5 %copy-start.6 = (bf16[768,32]{0,1:T(8,128)(2,1)S(1)}, bf16[768,32]{0,1:T(8,128)(2,1)}, u32[]{:S(2)}) copy-start(bf16[768,32]{0,1:T(8,128)(2,1)} %param.21) | copy-start | bytes 147460
Sparse Core Ops, SparseCore 0:
  273.1 274.0 all-reduce.3
  565.1 287.7 all-reduce.5
where the time goes:
time: 989 us
  blocking collectives  674 us (68%)
  waiting for transfers between devices  286 us (29%)
  between operations  14.3 us (1%)
    psum x1, waiting for transfers between devices, body(): lax.psum(jnp.dot(every, joined, preferred_element_type=jnp.float32), 'seq')  286 us
    psum x1, blocking collectives, body(): lax.psum((factor * local[1], factor[..., None] * local[2]), 'seq')  274 us
    pmax x1, blocking collectives, body(): highest = lax.pmax(local[0], 'seq')  262 us
    all_gather x1, blocking collectives, body(): return lax.all_gather(piece, 'seq', axis=2, tiled=True)  100 us
    unnamed x1, blocking collectives  24.7 us
  transfers between devices with their start and end apart: 2, of which 1 were waited for; matrix products, arithmetic and copies ran while one was open for 0% of the time, Pallas kernels for 0%

commit v1 on v0

--- a/solution.py
+++ b/solution.py
@@ -9,6 +9,11 @@
 HEAD_SIZE = 128
 NEG_FILL = -1e30
 EPSILON = 1e-06
+
+
+def gather_by_exchange(value, axis, dim):
+    copies = jnp.concatenate([value] * lax.axis_size(axis), axis=dim)
+    return lax.all_to_all(copies, axis, dim, dim, tiled=True)
 
 
 def partial_softmax(q, keys, values, valid):
@@ -69,7 +74,7 @@
     down = jnp.dot(hidden, w_down, preferred_element_type=jnp.float32)
     down = lax.psum_scatter(down.reshape(steps, -1, width), "req", scatter_dimension=1, tiled=True)
     piece = (lax.dynamic_slice_in_dim(stream, me * width, width, 2) + down).astype(jnp.bfloat16)
-    return lax.all_gather(piece, "seq", axis=2, tiled=True)
+    return gather_by_exchange(piece, "seq", 2)
 
 
 def solution(mesh):

time: 989 us -> 920 us (0.930)
  blocking collectives: 674 us -> 598 us
    all_gather x1 -> x0, blocking collectives: 100 us -> none  [body(): return lax.all_gather(piece, 'seq', axis=2, tiled=True)]
    all_to_all x0 -> x1, blocking collectives: none -> 24.5 us  [gather_by_exchange(): return lax.all_to_all(copies, axis, dim, dim, tiled=True)]
where the time goes in v1:
time: 920 us
  blocking collectives  598 us (65%)
  waiting for transfers between devices  286 us (31%)
  between operations  14.3 us (2%)
  local copies, waits for them, and re-layouts  12.2 us (1%)
    psum x1, waiting for transfers between devices, body(): lax.psum(jnp.dot(every, joined, preferred_element_type=jnp.float32), 'seq')  286 us
    psum x1, blocking collectives, body(): lax.psum((factor * local[1], factor[..., None] * local[2]), 'seq')  274 us
    pmax x1, blocking collectives, body(): highest = lax.pmax(local[0], 'seq')  262 us
    unnamed x1, blocking collectives  24.7 us
    all_to_all x1, blocking collectives, gather_by_exchange(): return lax.all_to_all(copies, axis, dim, dim, tiled=True)  24.5 us
  transfers between devices with their start and end apart: 2, of which 1 were waited for; matrix products, arithmetic and copies ran while one was open for 0% of the time, Pallas kernels for 0%

profile of v1, /device:TPU:8, one launch (start us, length us, event | category | flops | bytes accessed | tf_op | source)
XLA Modules:
  0.0 919.6 jit_solution(11777728891706719285)
XLA Ops:
  6.6 1.1 copy.123
  7.6 0.7 broadcast_compare_fusion
  8.4 1.5 fusion.27
  9.9 261.8 %pmax.7 = f32[8,8,8]{2,1,0:T(8,128)S(1)} all-reduce(f32[8,8,8]{2,1,0:T(8,128)S(1)} %get-tuple-element.10), channel_id=1, replica_groups=mesh['seq'=64,'req'=8] {'seq'}, use_global_device_ids=true, to_apply=%region_1.2 | all-reduce | flops 512 | bytes 4096 | tf_op jit(solution)/shard_map/pmax | solution.py:46
  271.6 0.3 convert_reduce_fusion
  271.9 1.0 convolution_multiply_fusion.1
  273.1 0.2 fusion.28
  273.4 0.8 dynamic-slice.2
  274.2 274.0 %psum.22 = f32[8,8,8]{2,1,0:T(8,128)S(1)} all-reduce(f32[8,8,8]{2,1,0:T(8,128)S(1)} %get-tuple-element.8), channel_id=1, replica_groups=mesh['seq'=64,'req'=8] {'seq'}, use_global_device_ids=true, to_apply=%region_5.6 | all-reduce | flops 512 | bytes 4096 | tf_op jit(solution)/shard_map/psum | solution.py:48
  548.3 1.4 fusion.3
  549.7 0.2 copy.128
  550.2 13.0 %all_gather.3 = bf16[4,64,32]{2,0,1:T(4,128)(2,1)S(1)} all-gather(bf16[4,8,32]{2,0,1:T(4,128)(2,1)S(1)} %copy.129), channel_id=1, replica_groups=mesh['seq'=64,'req'=8] {'req'}, dimensions={1}, use_global_device_ids=true | all-gather | bytes 18432 | tf_op jit(solution)/shard_map/all_gather | solution.py:70
  563.5 1.5 fusion.12
  565.0 1.3 dynamic-slice
  566.9 286.0 %all-reduce.6.cloned.1.call-done = f32[256,1536]{1,0:T(8,128)} async-done(((f32[256,1536]{1,0:T(8,128)}), f32[256,1536]{1,0:T(8,128)}) %all-reduce.6.cloned.1.call-update) | async-done | bytes 1572880 | tf_op jit(solution)/shard_map/psum | solution.py:72
  853.0 1.7 fusion.10
  854.7 0.1 reshape.72
  854.9 24.7 %all-reduce = f32[4,64,32]{2,0,1:T(4,128)S(1)} all-reduce(f32[4,64,32]{2,0,1:T(4,128)S(1)} %copy.131), channel_id=2, replica_groups=mesh['seq'=64,'req'=8] {'req'}, use_global_device_ids=true, to_apply=%region_9.10.clone | all-reduce | flops 8192 | bytes 65536
  879.7 0.3 concatenate.7
  880.1 1.3 copy.133
  881.4 2.3 reshape.74
  883.7 24.5 %all_to_all.5 = bf16[64,2,512]{2,1,0:T(2,128)(2,1)S(1)} all-to-all(bf16[64,2,512]{2,1,0:T(2,128)(2,1)S(1)} %reshape.74), channel_id=1, replica_groups=mesh['seq'=64,'req'=8] {'seq'}, dimensions={0} | all-to-all | bytes 262144 | tf_op jit(solution)/shard_map/all_to_all | solution.py:16
  908.2 2.4 reshape.75
  910.6 2.1 copy.134
  (36 shorter events, 1.0 us)
Async XLA Ops:
  6.5 265.4 %copy-start = (bf16[8,32,1024]{2,1,0:T(8,128)(2,1)S(1)}, bf16[8,32,1024]{2,1,0:T(8,128)(2,1)}, u32[]{:S(2)}) copy-start(bf16[8,32,1024]{2,1,0:T(8,128)(2,1)} %param.15) | copy-start | bytes 1572868
  6.5 541.8 %all-reduce.4.cloned.1.call-start = ((), (), s32[]{:S(2)}) async-start(), calls=%async_computation.1 | async-start | bytes 524288 | tf_op jit(solution)/shard_map/psum | solution.py:48
  6.5 266.5 %copy-start.4 = (bf16[4,8,1024]{2,1,0:T(8,128)(2,1)S(1)}, bf16[4,8,1024]{2,1,0:T(8,128)(2,1)}, u32[]{:S(2)}) copy-start(bf16[4,8,1024]{2,1,0:T(8,128)(2,1)} %param.12) | copy-start | bytes 196612
  9.8 538.5 %copy-start.5 = (bf16[4,8,1024]{2,1,0:T(8,128)(2,1)S(1)}, bf16[4,8,1024]{2,1,0:T(8,128)(2,1)}, u32[]{:S(2)}) copy-start(bf16[4,8,1024]{2,1,0:T(8,128)(2,1)} %param.13) | copy-start | bytes 196612
  273.0 580.0 %all-reduce.6.cloned.1.call-start = ((), (), s32[]{:S(2)}) async-start(), calls=%async_computation.2 | async-start | bytes 3145728 | tf_op jit(solution)/shard_map/psum | solution.py:72
  273.1 276.8 %copy-start.1 = (bf16[4,8,2048]{2,1,0:T(8,128)(2,1)S(1)}, bf16[4,8,2048]{2,1,0:T(8,128)(2,1)}, u32[]{:S(2)}) copy-start(bf16[4,8,2048]{2,1,0:T(8,128)(2,1)} %param.17) | copy-start | bytes 393220
  548.3 15.1 %copy-start.2 = (bf16[32,768]{1,0:T(8,128)(2,1)S(1)}, bf16[32,768]{1,0:T(8,128)(2,1)}, u32[]{:S(2)}) copy-start(bf16[32,768]{1,0:T(8,128)(2,1)} %param.20) | copy-start | bytes 147460
  548.3 15.1 %copy-start.3 = (bf16[32,768]{1,0:T(8,128)(2,1)S(1)}, bf16[32,768]{1,0:T(8,128)(2,1)}, u32[]{:S(2)}) copy-start(bf16[32,768]{1,0:T(8,128)(2,1)} %param.19) | copy-start | bytes 147460
  563.4 289.5 %copy-start.6 = (bf16[768,32]{0,1:T(8,128)(2,1)S(1)}, bf16[768,32]{0,1:T(8,128)(2,1)}, u32[]{:S(2)}) copy-start(bf16[768,32]{0,1:T(8,128)(2,1)} %param.21) | copy-start | bytes 147460
Sparse Core Ops, SparseCore 0:
  273.1 274.0 all-reduce.3
  565.1 287.7 all-reduce.5
